TPU v7x, 256 devices: a whole 4x4x8 slice. The times are simulated.
256 devices in a mesh: row: 32 (over y, z_lo, core), col: 8 (over x, z_hi).
Axes of the slice: x: 4, y: 4, z: 8 (z_hi: 2, z_lo: 4; z = z_hi * 4 + z_lo), core: 2. Of those that a mesh axis runs over, the one named last changes fastest.
Arguments:
- object_field: bfloat16 [2, 8192, 8192], P(None, 'row', 'col'), may hold values from -6 to 6
- probe: float32 [2, 2, 256, 256], replicated, may hold values from -5 to 5
- measured: bfloat16 [32, 8, 12, 256, 256], P('row', 'col'), may hold values from 0.3984375 to 4
- positions: int32 [32, 8, 12, 2], P('row', 'col'), may hold values from 0 to 1023, as said below
- counts: int32 [32, 8], P('row', 'col'), may hold values from 1 to 12, as said below
Outputs:
- object_grad: float32 [2, 8192, 8192], P(None, 'row', 'col')
- probe_grad: float32 [2, 2, 256, 256], replicated
Inputs may be any that keep to these rules, and one draw needn't show every extreme that they name: positions[i, j, s, 0] lies in 0 to 255 and positions[i, j, s, 1] in 0 to 1023 for every slot, live or not. `counts`: some tile has all 12 slots live.
All inputs are finite; a program needn't handle non-finite values.
Results may differ from a plain program's by a relative error of at most 0.0048.
The roundings to bfloat16 on the way count: a program that leaves them out, or rounds other values in their place, can miss the bound.
Values may be sent and summed in bfloat16 or wider, within the bound.
No kernel may reach another device: no remote copies, remote signals or barrier semaphores. Data moves between devices by JAX's collectives and lax.ppermute only.
A program may use at most 128 MiB of HBM per device.

v0:
```python
import jax
import jax.numpy as jnp
from jax import lax
from jax.sharding import PartitionSpec as P


def from_behind(x, axis, by):
    peers = lax.axis_size(axis)
    pairs = [(i, i + by) for i in range(peers) if 0 <= i + by < peers]
    return lax.ppermute(x, axis, pairs)


def dft_tables(size, sign):
    index = jnp.arange(size, dtype=jnp.int32)
    phase = index[:, None] * index[None, :] % size
    angle = 2.0 * jnp.pi / size * phase.astype(jnp.float32)
    cosine = jnp.cos(angle) / jnp.sqrt(jnp.float32(size))
    sine = sign * jnp.sin(angle) / jnp.sqrt(jnp.float32(size))
    left = jnp.stack([jnp.stack([cosine, sine], 0), jnp.stack([-sine, cosine], 0)], 0)
    right = jnp.stack([jnp.stack([cosine, -sine], 1), jnp.stack([sine, cosine], 1)], 0)
    return (left.astype(jnp.bfloat16), right.astype(jnp.bfloat16))


def transform(field, left, right):
    half = jnp.einsum("ocij,mcjk->moik", left, field, preferred_element_type=jnp.float32).astype(
        jnp.bfloat16
    )
    return jnp.einsum("mcij,cjdk->mdik", half, right, preferred_element_type=jnp.float32)


def position_terms(patch, frame, probe, tables):
    fwd_left, fwd_right, inv_left, inv_right = tables
    obj = patch.astype(jnp.float32)
    obj_re, obj_im = (obj[0], obj[1])
    pro_re, pro_im = (probe[:, 0], probe[:, 1])
    wave = jnp.stack(
        [pro_re * obj_re - pro_im * obj_im, pro_re * obj_im + pro_im * obj_re], 1
    ).astype(jnp.bfloat16)
    spectrum = transform(wave, fwd_left, fwd_right)
    intensity = jnp.sum(spectrum * spectrum, axis=(0, 1))
    amplitude = jnp.sqrt(intensity + 1.0)
    factor = 1.0 - frame.astype(jnp.float32) / amplitude
    weighted = (spectrum * factor).astype(jnp.bfloat16)
    back = transform(weighted, inv_left, inv_right)
    back_re, back_im = (back[:, 0], back[:, 1])
    obj_grad = jnp.stack(
        [
            jnp.sum(pro_re * back_re + pro_im * back_im, 0),
            jnp.sum(pro_re * back_im - pro_im * back_re, 0),
        ],
        0,
    )
    probe_part = jnp.stack(
        [obj_re * back_re + obj_im * back_im, obj_re * back_im - obj_im * back_re], 1
    )
    return (obj_grad, probe_part)


def add_patch(grad, patch, row_at, col_at):
    zero = jnp.zeros((), jnp.int32)
    size = patch.shape[-1]
    old = lax.dynamic_slice(grad, (zero, row_at, col_at), (2, size, size))
    return lax.dynamic_update_slice(grad, old + patch, (zero, row_at, col_at))


def body(object_field, probe, measured, positions, counts):
    size = probe.shape[-1]
    tile_rows = object_field.shape[1]
    tile_cols = object_field.shape[2]
    slots = measured.shape[2]
    frames = measured[0, 0]
    offsets = positions[0, 0]
    count = counts[0, 0]
    fwd_left, fwd_right = dft_tables(size, 1.0)
    inv_left, inv_right = dft_tables(size, -1.0)
    tables = (fwd_left, fwd_right, inv_left, inv_right)
    zero = jnp.zeros((), jnp.int32)
    below = from_behind(object_field, "row", -1)
    tall = jnp.concatenate([object_field, below], 1)
    strip = from_behind(tall[:, :, :size], "col", -1)
    extended = jnp.concatenate([tall, strip], 2)
    grad = jnp.zeros(extended.shape, jnp.float32)
    probe_sum = jnp.zeros(probe.shape, jnp.float32)

    def own_step(index, carry):
        grad_now, probe_now = carry
        row_at = offsets[index, 0]
        col_at = offsets[index, 1]
        patch = lax.dynamic_slice(extended, (zero, row_at, col_at), (2, size, size))
        obj_grad, probe_part = position_terms(patch, frames[index], probe, tables)
        return (add_patch(grad_now, obj_grad, row_at, col_at), probe_now + probe_part)

    grad, probe_sum = lax.fori_loop(0, count, own_step, (grad, probe_sum))
    total_slots = slots * lax.axis_size("row") * lax.axis_size("col")
    probe_grad = lax.psum(probe_sum / jnp.sqrt(jnp.float32(total_slots)), ("row", "col"))
    strip_grad = from_behind(grad[:, :, tile_cols:], "col", 1)
    grad = grad[:, :, :tile_cols]
    grad = grad.at[:, :, :size].add(strip_grad)
    band_grad = from_behind(grad[:, tile_rows:, :], "row", 1)
    grad = grad[:, :tile_rows, :]
    object_grad = grad.at[:, :size, :].add(band_grad)
    return (object_grad, probe_grad)


def solution(mesh):
    placed = (
        P(None, "row", "col"),
        P(),
        P("row", "col", None, None, None),
        P("row", "col", None, None),
        P("row", "col"),
    )
    return jax.shard_map(
        body, mesh=mesh, in_specs=placed, out_specs=(P(None, "row", "col"), P()), check_vma=False
    )
```

profile of v0, /device:TPU:2, one launch (start us, length us, event | category | flops | bytes accessed | tf_op | source)
XLA Modules:
  0.0 633.6 jit_solution(1954523480377900245)
XLA Ops:
  7.2 1.4 collective-permute-start
  8.6 1.0 multiply_convert_fusion.6
  10.6 1.0 multiply_convert_fusion.4
  12.6 1.1 multiply_convert_fusion.1
  13.7 1.0 negate_convert_fusion
  15.1 1.3 copy-done.2
  17.3 9.1 %collective-permute-start.1 = (bf16[2,512,256]{2,1,0:T(8,128)(2,1)}, bf16[2,512,256]{2,1,0:T(8,128)(2,1)S(1)}, u32[]{:S(2)}, u32[]{:S(2)}) collective-permute-start(bf16[2,512,256]{2,1,0:T(8,128)(2,1)} %slice.87), channel_id=1, source_target_pairs={{1,0},{2,1},{3,2},{4,3},{5,4},{6,5},{7,6},{9,8},{10,9},{11,10},{12... | collective-permute-start | bytes 1572872 | tf_op jit(solution)/shard_map/ppermute | solution.py:10
  26.3 1.6 negate_convert_fusion.3
  30.0 1.1 pad_maximum_fusion.1
  31.2 2.5 collective-permute-done.1
  33.7 1.7 pad_maximum_fusion
  35.4 1.1 broadcast_in_dim.5
  36.4 2.6 broadcast_in_dim.4
  39.1 24.3 %while.15 = (s32[]{:T(128)}, f32[2,512,1280]{2,1,0:T(8,128)}, f32[2,2,256,256]{3,2,1,0:T(8,128)}, s32[]{:T(128)}, s32[12,2]{0,1:T(2,128)S(1)}, /*index=5*/f32[2,...) while((s32[]{:T(128)}, f32[2,512,1280]{2,1,0:T(8,128)}, ...), condition=%wide.region_4.5_spmd, body=%wide.region_0.4_spmd.sunk | while | flops 1080229888 | bytes 25035120 | solution.py:93
  44.7 1.2 dynamic-slice_convert_fusion.2
  46.1 2.8 multiply_reduce_fusion.2
  49.8 2.1 convolution_bitcast_fusion.5
  52.2 1.4 maximum_add_fusion.4
  53.7 2.3 maximum_add_fusion.5
  56.0 6.8 %dynamic_update_slice.4 = f32[2,512,1280]{2,1,0:T(8,128)} dynamic-update-slice(f32[2,512,1280]{2,1,0:T(8,128)} %get-tuple-element.280, f32[2,256,256]{2,1,0:T(8,128)S(1)} %maximum_add_fusion.4, s32[]{:T(128)} %constant.104.clone.1..sunk, s32[]{:T(128)S(6)} %select_n.140, s32[]{:T(128)S(6)} %select_n.141) | dynamic-update-slice | bytes 1048580 | tf_op jit(solution)/shard_map/while/body/dynamic_update_slice | solution.py:63
  63.4 1.3 slice.80
  64.7 100.0 %collective-permute-start.2 = (f32[2,512,256]{2,1,0:T(8,128)S(1)}, f32[2,512,256]{2,1,0:T(8,128)S(1)}, u32[]{:S(2)}, u32[]{:S(2)}) collective-permute-start(f32[2,512,256]{2,1,0:T(8,128)S(1)} %slice.80), channel_id=1, source_target_pairs={{0,1},{1,2},{2,3},{3,4},{4,5},{5,6},{6,7},{8,9},{9,10},{10,11},{11... | collective-permute-start | bytes 3145736 | tf_op jit(solution)/shard_map/ppermute | solution.py:10
  164.8 2.5 slice.78
  167.3 46.9 %collective-permute-done.2 = f32[2,512,256]{2,1,0:T(8,128)S(1)} collective-permute-done((f32[2,512,256]{2,1,0:T(8,128)S(1)}, f32[2,512,256]{2,1,0:T(8,128)S(1)}, u32[]{:S(2)}, u32[]{:S(2)}) %collective-permute-start.2) | collective-permute-done | bytes 1048608 | tf_op jit(solution)/shard_map/ppermute | solution.py:10
  214.2 1.4 add_dynamic-update-slice_fusion
  215.6 1.9 copy-done.1
  217.5 1.5 slice.89
  219.0 2.6 collective-permute-start.3
  221.6 2.3 broadcast_multiply_fusion
  224.4 4.1 slice_add_fusion
  228.5 396.0 %all-reduce.2.cloned.1.call-done = f32[2,2,256,256]{3,2,1,0:T(8,128)} async-done(((f32[2,2,256,256]{3,2,1,0:T(8,128)}), f32[2,2,256,256]{3,2,1,0:T(8,128)}) %all-reduce.2.cloned.1.call-update) | async-done | bytes 1048592 | tf_op jit(solution)/shard_map/psum | solution.py:95
  624.5 2.3 copy.30
  (34 shorter events, 7.8 us)
Async XLA Ops:
  7.2 7.7 %copy-start.4 = (bf16[2,256,1024]{2,1,0:T(8,128)(2,1)S(1)}, bf16[2,256,1024]{2,1,0:T(8,128)(2,1)}, u32[]{:S(2)}) copy-start(bf16[2,256,1024]{2,1,0:T(8,128)(2,1)} %param.13) | copy-start | bytes 3145732
  7.2 617.3 %all-reduce.2.cloned.1.call-start = ((), (), s32[]{:S(2)}) async-start(), calls=%async_computation | async-start | bytes 2097152 | tf_op jit(solution)/shard_map/psum | solution.py:95
  7.2 7.8 %collective-permute-start = (bf16[2,256,1024]{2,1,0:T(8,128)(2,1)}, bf16[2,256,1024]{2,1,0:T(8,128)(2,1)S(1)}, u32[]{:S(2)}, u32[]{:S(2)}) collective-permute-start(bf16[2,256,1024]{2,1,0:T(8,128)(2,1)} %param.13), channel_id=1, source_target_pairs={{8,0},{16,8},{24,16},{32,24},{40,32},{48,40},{56,48},{64,56},{72,6... | collective-permute-start | bytes 3145736 | tf_op jit(solution)/shard_map/ppermute | solution.py:10
  15.1 1.3 copy-start.2
  17.3 16.4 %collective-permute-start.1 = (bf16[2,512,256]{2,1,0:T(8,128)(2,1)}, bf16[2,512,256]{2,1,0:T(8,128)(2,1)S(1)}, u32[]{:S(2)}, u32[]{:S(2)}) collective-permute-start(bf16[2,512,256]{2,1,0:T(8,128)(2,1)} %slice.87), channel_id=1, source_target_pairs={{1,0},{2,1},{3,2},{4,3},{5,4},{6,5},{7,6},{9,8},{10,9},{11,10},{12... | collective-permute-start | bytes 1572872 | tf_op jit(solution)/shard_map/ppermute | solution.py:10
  28.0 5.7 copy-start.3
  36.4 2.7 copy-start
  36.4 2.7 copy-start.7
  39.9 9.0 %copy-start.5 = (bf16[2,256,2,256]{3,1,0,2:T(8,128)(2,1)}, bf16[2,256,2,256]{3,1,0,2:T(8,128)(2,1)S(1)}, u32[]{:S(2)}) copy-start(bf16[2,256,2,256]{3,1,0,2:T(8,128)(2,1)S(1)} %get-tuple-element.304) | copy-start | bytes 1572868 | tf_op jit(solution)/shard_map/while
  52.2 10.6 %copy-start.6 = (bf16[2,256,2,256]{3,1,0,2:T(8,128)(2,1)S(1)}, bf16[2,256,2,256]{3,1,0,2:T(8,128)(2,1)}, u32[]{:S(2)}) copy-start(bf16[2,256,2,256]{3,1,0,2:T(8,128)(2,1)} %copy-done.5) | copy-start | bytes 1572868 | tf_op jit(solution)/shard_map/while
  64.7 149.4 %collective-permute-start.2 = (f32[2,512,256]{2,1,0:T(8,128)S(1)}, f32[2,512,256]{2,1,0:T(8,128)S(1)}, u32[]{:S(2)}, u32[]{:S(2)}) collective-permute-start(f32[2,512,256]{2,1,0:T(8,128)S(1)} %slice.80), channel_id=1, source_target_pairs={{0,1},{1,2},{2,3},{3,4},{4,5},{5,6},{6,7},{8,9},{9,10},{10,11},{11... | collective-permute-start | bytes 3145736 | tf_op jit(solution)/shard_map/ppermute | solution.py:10
  215.6 1.9 copy-start.1
  219.0 5.4 collective-permute-start.3
Sparse Core Ops, SparseCore 0:
  224.1 400.3 all-reduce.1
where the time goes:
time: 639 us; the launch traced here: 634 us
  waiting for transfers between devices  446 us (70%)
  starting transfers between devices  113 us (18%)
  other arithmetic  26.8 us (4%)
  local copies, waits for them, and re-layouts  23.1 us (4%)
  between operations  14.2 us (2%)
    psum x1, waiting for transfers between devices, body(): lax.psum(probe_sum / jnp.sqrt(jnp.float32(total_slots)), ('row', 'col'))  396 us
    ppermute x4, starting transfers between devices, from_behind(): return lax.ppermute(x, axis, pairs)  113 us
    ppermute x4, waiting for transfers between devices, from_behind(): return lax.ppermute(x, axis, pairs)  49.8 us
  transfers between devices with their start and end apart: 5, of which 4 were waited for; matrix products, arithmetic and copies ran while one was open for 3% of the time, Pallas kernels for 0%

commit v1 on v0

--- a/solution.py
+++ b/solution.py
@@ -1,7 +1,16 @@
+import functools
 import jax
 import jax.numpy as jnp
 from jax import lax
 from jax.sharding import PartitionSpec as P
+
+
+def paths_watch(content, axis_key, peer_axis):
+    y = lax.psum(lax.psum(content, axis_name=axis_key), peer_axis)
+    return y
+
+
+_watch_block = functools.partial(paths_watch, axis_key="col", peer_axis="row")
 
 
 def from_behind(x, axis, by):
@@ -92,7 +101,7 @@
 
     grad, probe_sum = lax.fori_loop(0, count, own_step, (grad, probe_sum))
     total_slots = slots * lax.axis_size("row") * lax.axis_size("col")
-    probe_grad = lax.psum(probe_sum / jnp.sqrt(jnp.float32(total_slots)), ("row", "col"))
+    probe_grad = _watch_block(probe_sum / jnp.sqrt(jnp.float32(total_slots)))
     strip_grad = from_behind(grad[:, :, tile_cols:], "col", 1)
     grad = grad[:, :, :tile_cols]
     grad = grad.at[:, :, :size].add(strip_grad)

time: 639 us -> 800 us (1.25)
  waiting for transfers between devices: 446 us -> 608 us
    psum x1 -> x2, waiting for transfers between devices: 396 us -> 560 us  [paths_watch(): y = lax.psum(lax.psum(content, axis_name=axis_key), peer_axis)]
  transfers between devices with their start and end apart: 5 -> 6, of which waited for: 4 -> 4; matrix products, arithmetic and copies ran while one was open for 3% -> 3% of each run, Pallas kernels for 0% -> 0%
where the time goes in v1:
time: 800 us; the launch traced here: 793 us
  waiting for transfers between devices  608 us (76%)
  starting transfers between devices  111 us (14%)
  other arithmetic  27.1 us (3%)
  local copies, waits for them, and re-layouts  22.5 us (3%)
  between operations  14.2 us (2%)
    psum x2, waiting for transfers between devices, paths_watch(): y = lax.psum(lax.psum(content, axis_name=axis_key), peer_axis)  560 us
    ppermute x4, starting transfers between devices, from_behind(): return lax.ppermute(x, axis, pairs)  111 us
    ppermute x4, waiting for transfers between devices, from_behind(): return lax.ppermute(x, axis, pairs)  48.4 us
  transfers between devices with their start and end apart: 6, of which 4 were waited for; matrix products, arithmetic and copies ran while one was open for 3% of the time, Pallas kernels for 0%

profile of v1, /device:TPU:2, one launch (start us, length us, event | category | flops | bytes accessed | tf_op | source)
XLA Modules:
  0.0 792.8 jit_solution(5354849973903325964)
XLA Ops:
  7.2 1.4 collective-permute-start
  8.6 1.0 multiply_convert_fusion.6
  10.6 1.0 multiply_convert_fusion.4
  12.6 1.1 multiply_convert_fusion.1
  13.7 1.0 negate_convert_fusion
  15.9 9.1 %collective-permute-start.1 = (bf16[2,512,256]{2,1,0:T(8,128)(2,1)}, bf16[2,512,256]{2,1,0:T(8,128)(2,1)}, u32[]{:S(2)}, u32[]{:S(2)}) collective-permute-start(bf16[2,512,256]{2,1,0:T(8,128)(2,1)} %slice.87), channel_id=1, source_target_pairs={{1,0},{2,1},{3,2},{4,3},{5,4},{6,5},{7,6},{9,8},{10,9},{11,10},{12... | collective-permute-start | bytes 1572872 | tf_op jit(solution)/shard_map/ppermute | solution.py:19
  25.0 1.7 negate_convert_fusion.3
  29.5 1.2 pad_maximum_fusion.1
  30.7 1.8 collective-permute-done.1
  32.5 2.7 pad_maximum_fusion
  35.2 1.1 broadcast_in_dim.5
  36.3 2.6 broadcast_in_dim.4
  38.9 24.0 %while.15 = (s32[]{:T(128)}, f32[2,512,1280]{2,1,0:T(8,128)}, f32[2,2,256,256]{3,2,1,0:T(8,128)}, s32[]{:T(128)}, s32[12,2]{0,1:T(2,128)S(1)}, /*index=5*/f32[2,...) while((s32[]{:T(128)}, f32[2,512,1280]{2,1,0:T(8,128)}, ...), condition=%wide.region_4.5_spmd, body=%wide.region_0.4_spmd.sunk | while | flops 1080229888 | bytes 22937948 | solution.py:102
  44.2 1.2 dynamic-slice_convert_fusion.2
  45.6 2.8 multiply_reduce_fusion.2
  49.4 2.1 convolution_bitcast_fusion.5
  51.7 1.4 maximum_add_fusion.4
  53.2 2.3 maximum_add_fusion.5
  55.5 6.8 dynamic_update_slice.4
  62.9 1.3 slice.80
  64.2 98.8 %collective-permute-start.2 = (f32[2,512,256]{2,1,0:T(8,128)S(1)}, f32[2,512,256]{2,1,0:T(8,128)S(1)}, u32[]{:S(2)}, u32[]{:S(2)}) collective-permute-start(f32[2,512,256]{2,1,0:T(8,128)S(1)} %slice.80), channel_id=1, source_target_pairs={{0,1},{1,2},{2,3},{3,4},{4,5},{5,6},{6,7},{8,9},{9,10},{10,11},{11... | collective-permute-start | bytes 3145736 | tf_op jit(solution)/shard_map/ppermute | solution.py:19
  163.0 2.5 slice.78
  165.6 46.6 %collective-permute-done.2 = f32[2,512,256]{2,1,0:T(8,128)S(1)} collective-permute-done((f32[2,512,256]{2,1,0:T(8,128)S(1)}, f32[2,512,256]{2,1,0:T(8,128)S(1)}, u32[]{:S(2)}, u32[]{:S(2)}) %collective-permute-start.2) | collective-permute-done | bytes 1048608 | tf_op jit(solution)/shard_map/ppermute | solution.py:19
  212.2 1.4 add_dynamic-update-slice_fusion
  213.6 1.9 copy-done.1
  215.5 1.5 slice.89
  217.0 1.4 collective-permute-start.3
  218.4 2.3 broadcast_multiply_fusion
  220.8 281.9 %all-reduce.3.cloned.1.call-done = f32[2,2,256,256]{3,2,1,0:T(8,128)} async-done(((f32[2,2,256,256]{3,2,1,0:T(8,128)}), f32[2,2,256,256]{3,2,1,0:T(8,128)}) %all-reduce.3.cloned.1.call-update) | async-done | bytes 1048592 | tf_op jit(solution)/shard_map/psum | solution.py:9
  502.7 3.3 slice_add_fusion
  506.0 277.6 %all-reduce.5.cloned.1.call-done = f32[2,2,256,256]{3,2,1,0:T(8,128)} async-done(((f32[2,2,256,256]{3,2,1,0:T(8,128)}), f32[2,2,256,256]{3,2,1,0:T(8,128)}) %all-reduce.5.cloned.1.call-update) | async-done | bytes 1048592 | tf_op jit(solution)/shard_map/psum | solution.py:9
  783.6 2.3 copy.31
  (33 shorter events, 8.2 us)
Async XLA Ops:
  7.2 495.5 %all-reduce.3.cloned.1.call-start = ((), (), s32[]{:S(2)}) async-start(), calls=%async_computation | async-start | bytes 2097152 | tf_op jit(solution)/shard_map/psum | solution.py:9
  7.2 7.7 copy-start.2
  7.2 7.8 collective-permute-start
  15.9 16.6 %collective-permute-start.1 = (bf16[2,512,256]{2,1,0:T(8,128)(2,1)}, bf16[2,512,256]{2,1,0:T(8,128)(2,1)}, u32[]{:S(2)}, u32[]{:S(2)}) collective-permute-start(bf16[2,512,256]{2,1,0:T(8,128)(2,1)} %slice.87), channel_id=1, source_target_pairs={{1,0},{2,1},{3,2},{4,3},{5,4},{6,5},{7,6},{9,8},{10,9},{11,10},{12... | collective-permute-start | bytes 1572872 | tf_op jit(solution)/shard_map/ppermute | solution.py:19
  36.3 2.7 copy-start
  36.3 2.7 copy-start.3
  36.3 2.7 copy-start.5
  51.7 10.5 %copy-start.4 = (bf16[2,256,2,256]{3,1,0,2:T(8,128)(2,1)S(1)}, bf16[2,256,2,256]{3,1,0,2:T(8,128)(2,1)}, u32[]{:S(2)}) copy-start(bf16[2,256,2,256]{3,1,0,2:T(8,128)(2,1)} %get-tuple-element.345) | copy-start | bytes 1572868 | tf_op jit(solution)/shard_map/while
  64.2 148.0 %collective-permute-start.2 = (f32[2,512,256]{2,1,0:T(8,128)S(1)}, f32[2,512,256]{2,1,0:T(8,128)S(1)}, u32[]{:S(2)}, u32[]{:S(2)}) collective-permute-start(f32[2,512,256]{2,1,0:T(8,128)S(1)} %slice.80), channel_id=1, source_target_pairs={{0,1},{1,2},{2,3},{3,4},{4,5},{5,6},{6,7},{8,9},{9,10},{10,11},{11... | collective-permute-start | bytes 3145736 | tf_op jit(solution)/shard_map/ppermute | solution.py:19
  213.6 2.0 copy-start.1
  217.0 285.7 %collective-permute-start.3 = (f32[2,256,1024]{2,1,0:T(8,128)}, f32[2,256,1024]{2,1,0:T(8,128)S(1)}, u32[]{:S(2)}, u32[]{:S(2)}) collective-permute-start(f32[2,256,1024]{2,1,0:T(8,128)} %slice.89), channel_id=1, source_target_pairs={{0,8},{8,16},{16,24},{24,32},{32,40},{40,48},{48,56},{56,64},{64,7... | collective-permute-start | bytes 6291464 | tf_op jit(solution)/shard_map/ppermute | solution.py:19
  220.8 562.9 %all-reduce.5.cloned.1.call-start = ((), (), s32[]{:S(2)}) async-start(), calls=%async_computation.1 | async-start | bytes 2097152 | tf_op jit(solution)/shard_map/psum | solution.py:9
Sparse Core Ops, SparseCore 0:
  220.9 281.7 all-reduce.2
  505.3 278.3 all-reduce.4
